TPU v7x, 32 devices: a whole 2x2x4 slice. The times are simulated.
32 devices in a mesh: occ: 4 (over z), vir: 8 (over y, x, core).
Axes of the slice: x: 2, y: 2, z: 4, core: 2. Of those that a mesh axis runs over, the one named last changes fastest.
Arguments:
- amplitudes: float32 [64, 1441792], P(None, ('occ', 'vir')), may hold values from -6 to 6
- slab: float32 [128, 1441792], P(None, ('occ', 'vir')), may hold values from -0.0048828125 to 0.0048828125
- mirror: int32 [128], replicated, may hold values from 0 to 127, as said below
Outputs:
- ladder: float32 [64, 128], P('occ')
Inputs may be any that keep to these rules, and one draw needn't show every extreme that they name: mirror pairs the rows: mirror[mirror[m]] = m and mirror[m] != m for every m.
All inputs are finite; a program needn't handle non-finite values.
Results may differ from a plain program's by a relative error of at most 0.000086.
Values sent between devices are 32-bit elements; how exact they have to be, the bound alone decides.
A program may use at most 128 MiB of HBM per device.

v0:
```python
import jax
import jax.numpy as jnp
from jax import lax
from jax.sharding import PartitionSpec as P


def contract(left, right):
    return lax.dot_general(
        left,
        right,
        (((1,), (1,)), ((), ())),
        precision=lax.Precision.HIGHEST,
        preferred_element_type=jnp.float32,
    )


def per_device(amplitudes, slab, mirror):
    own_rows = amplitudes.shape[0] // lax.axis_size("occ")
    partial_sum = contract(amplitudes, slab)
    summed = lax.psum(partial_sum, ("occ", "vir"))
    totals = lax.dynamic_slice_in_dim(summed, lax.axis_index("occ") * own_rows, own_rows, 0)
    return totals - jnp.take(totals, mirror, axis=1)


def solution(mesh):
    placed = (P(None, ("occ", "vir")), P(None, ("occ", "vir")), P())
    return jax.shard_map(
        per_device, mesh=mesh, in_specs=placed, out_specs=P("occ", None), check_vma=False
    )
```

profile of v0, /device:TPU:0, one launch (start us, length us, event | category | flops | bytes accessed | tf_op | source)
XLA Modules:
  0.0 71.5 jit_solution(2949817621040517710)
XLA Ops:
  0.0 0.0 copy-start
  0.0 27.9 %fusion = f32[64,128]{1,0:T(8,128)S(1)} fusion(f32[64,45056]{1,0:T(8,128)} %param.3, f32[128,45056]{1,0:T(8,128)} %param.4), kind=kOutput, calls=%fused_computation.6 | convolution fusion | flops 4429185024 | bytes 34635776 | tf_op jit(solution)/shard_map/dot_general | solution.py:8
  27.9 42.1 %psum.7 = f32[64,128]{1,0:T(8,128)S(1)} all-reduce(f32[64,128]{1,0:T(8,128)S(1)} %fusion), channel_id=1, replica_groups=mesh['occ'=4,'vir'=8] {'occ','vir'}, use_global_device_ids=true, to_apply=%region_0.0 | all-reduce | flops 8192 | bytes 65536 | tf_op jit(solution)/shard_map/psum | solution.py:20
  70.0 0.1 copy.4
  70.1 0.0 copy-done
  70.2 0.6 gather_fusion
  70.9 0.6 bitcast_subtract_fusion
  (5 shorter events, 0.1 us)
Async XLA Ops:
  0.0 70.1 %copy-start = (s32[128]{0:T(128)S(1)}, s32[128]{0:T(128)}, u32[]{:S(2)}) copy-start(s32[128]{0:T(128)} %param.5) | copy-start | bytes 1540
where the time goes:
time: 71.7 us; the launch traced here: 71.5 us
  blocking collectives  42.1 us (59%)
  matrix products  27.9 us (39%)
  local copies, waits for them, and re-layouts  0.81 us (1%)
    psum x1, blocking collectives, per_device(): summed = lax.psum(partial_sum, ('occ', 'vir'))  42.1 us
    dot_general x1, matrix products, contract(): lax.dot_general(left, right, (((1,), (1,)), ((), ())), precision=lax.Prec...  27.9 us

commit v1 on v0

--- a/solution.py
+++ b/solution.py
@@ -17,7 +17,7 @@
 def per_device(amplitudes, slab, mirror):
     own_rows = amplitudes.shape[0] // lax.axis_size("occ")
     partial_sum = contract(amplitudes, slab)
-    summed = lax.psum(partial_sum, ("occ", "vir"))
+    summed = jnp.sum(lax.all_gather(partial_sum, ("occ", "vir")), axis=0)
     totals = lax.dynamic_slice_in_dim(summed, lax.axis_index("occ") * own_rows, own_rows, 0)
     return totals - jnp.take(totals, mirror, axis=1)
 

time: 71.7 us -> 101 us (1.41)
  waiting for transfers between devices: 0 us -> 56.4 us
  blocking collectives: 42.1 us -> 0 us
  between operations: 0.05 us -> 13.4 us
    all_gather x0 -> x1, waiting for transfers between devices: none -> 56.4 us  [per_device(): summed = jnp.sum(lax.all_gather(partial_sum, ('occ', 'vir')), axis=0)]
    psum x1 -> x0, blocking collectives: 42.1 us -> none  [per_device(): summed = lax.psum(partial_sum, ('occ', 'vir'))]
    reduce_sum x0 -> x1, other arithmetic: none -> 1.29 us  [per_device(): summed = jnp.sum(lax.all_gather(partial_sum, ('occ', 'vir')), axis=0)]
  transfers between devices with their start and end apart: 0 -> 1, of which waited for: 0 -> 1; matrix products, arithmetic and copies ran while one was open for 0% -> 0% of each run, Pallas kernels for 0% -> 0%
where the time goes in v1:
time: 101 us
  waiting for transfers between devices  56.4 us (56%)
  matrix products  28.5 us (28%)
  between operations  13.4 us (13%)
  local copies, waits for them, and re-layouts  1.43 us (1%)
  other arithmetic  1.39 us (1%)
    all_gather x1, waiting for transfers between devices, per_device(): summed = jnp.sum(lax.all_gather(partial_sum, ('occ', 'vir')), axis=0)  56.4 us
    dot_general x1, matrix products, contract(): lax.dot_general(left, right, (((1,), (1,)), ((), ())), precision=lax.Prec...  28.5 us
  transfers between devices with their start and end apart: 1, of which 1 were waited for; matrix products, arithmetic and copies ran while one was open for 0% of the time, Pallas kernels for 0%

profile of v1, /device:TPU:0, one launch (start us, length us, event | category | flops | bytes accessed | tf_op | source)
XLA Modules:
  0.0 101.2 jit_solution(1713138148755534108)
XLA Ops:
  6.5 0.0 copy-start
  6.5 0.0 all-gather.3.cloned.1.call-start
  6.5 28.5 %fusion = f32[64,128]{1,0:T(8,128)} fusion(f32[64,45056]{1,0:T(8,128)} %param.3, f32[128,45056]{1,0:T(8,128)} %param.4), kind=kOutput, calls=%fused_computation.6 | convolution fusion | flops 4429185024 | bytes 34635776 | tf_op jit(solution)/shard_map/dot_general | solution.py:8
  35.0 0.0 all-gather.3.cloned.1.call-update
  35.0 0.0 copy-done
  35.1 56.4 %all-gather.3.cloned.1.call-done = f32[2048,128]{1,0:T(8,128)} async-done(((f32[64,128]{1,0:T(8,128)}), f32[2048,128]{1,0:T(8,128)}) %all-gather.3.cloned.1.call-update) | async-done | bytes 1048592 | tf_op jit(solution)/shard_map/all_gather | solution.py:20
  91.5 1.3 %reduce_sum.9 = f32[64,128]{1,0:T(8,128)S(1)} reduce(f32[32,64,128]{2,1,0:T(8,128)} %bitcast.5, f32[]{:T(128)} %constant.8.clone.1), dimensions={0}, to_apply=%region_0.0 | reduce | flops 253952 | bytes 1081348 | tf_op jit(solution)/shard_map/reduce_sum | solution.py:20
  92.8 0.1 copy.7
  92.9 0.6 gather_fusion
  93.6 0.1 bitcast_subtract_fusion
  93.7 0.7 copy.6
  (4 shorter events, 0.0 us)
Async XLA Ops:
  6.5 28.5 %copy-start = (s32[128]{0:T(128)S(1)}, s32[128]{0:T(128)}, u32[]{:S(2)}) copy-start(s32[128]{0:T(128)} %param.5) | copy-start | bytes 1540
  6.5 85.0 %all-gather.3.cloned.1.call-start = ((), (), s32[]{:S(2)}) async-start(), calls=%async_computation | async-start | bytes 1081344 | tf_op jit(solution)/shard_map/all_gather | solution.py:20
Sparse Core Ops, SparseCore 0:
  35.2 56.3 all-gather.2
